TPU v7x, 32 devices: a whole 2x2x4 slice. The times are simulated.
32 devices in a mesh: row: 4 (over z), col: 8 (over y, x, core).
Axes of the slice: x: 2, y: 2, z: 4, core: 2. Of those that a mesh axis runs over, the one named last changes fastest.
Arguments:
- coords: float32 [3, 4096], P(None, ('row', 'col')), may hold values from -1 to 1
- residual_in: float32 [4096, 512], P(('row', 'col')), may hold values from -6 to 6
- link_mask: int32 [32, 2], P(('row', 'col')), may hold values 0 or 1
- compress: float32 [4096, 256], P(('row', 'col')), may hold values from -0.5 to 0.5
- expand: float32 [4096, 256], P(('row', 'col')), may hold values from -0.375 to 0.375
- level_gain: float32 [32, 1280], P(('row', 'col')), may hold values from 0.5 to 1.5
- level_couple: float32 [8192, 1280], P(('row', 'col')), may hold values from -0.1875 to 0.1875
- partner_perm: int32 [32, 5, 256], P(('row', 'col')), may hold values from 0 to 255, each once within a row
Outputs:
- new_residual: float32 [4096, 512], P(('row', 'col'))
- res_norms: float32 [512], replicated
Inputs may be any that keep to these rules, and one draw needn't show every extreme that they name: `partner_perm`: each row of 256 entries names every number once.
All inputs are finite; a program needn't handle non-finite values. No bound on the sum of `link_mask` on one device may be relied on, other than what follows from the above.
Results may differ from a plain program's by a relative error of at most 0.0003.
Values sent between devices are 32-bit elements; how exact they have to be, the bound alone decides.
A program may use at most 64 MiB of HBM per device.

v0:
```python
import functools

import jax
import jax.numpy as jnp
from jax import lax
from jax.experimental import pallas as pl
from jax.experimental.pallas import tpu as pltpu
from jax.sharding import PartitionSpec as P

ROW_LEVELS = 2
COL_LEVELS = 3


WAVENUM = 6.0
SOFTEN = 0.01
LANES = 128
SUB = 8
STREAMS = 2
MESH = pl.DeviceIdType.MESH


def from_behind(block, axis, distance):
    devices = range(lax.axis_size(axis))
    route = [(i - distance, i) for i in devices if i - distance in devices]
    return lax.ppermute(block, axis, route)


def from_partner(block, axis, distance):
    count = lax.axis_size(axis)
    route = []
    for low in range(count):
        high = low | 1 << distance
        if high != low and high < count:
            route += [(low, high), (high, low)]
    return lax.ppermute(block, axis, route)


def kernel_tile(own_xyz, other_xyz):
    dist_sq = (own_xyz[0][:, None] - other_xyz[0][None, :]) ** 2
    dist_sq = dist_sq + (own_xyz[1][:, None] - other_xyz[1][None, :]) ** 2
    dist_sq = dist_sq + (own_xyz[2][:, None] - other_xyz[2][None, :]) ** 2
    return jnp.cos(WAVENUM * jnp.sqrt(dist_sq)) / jnp.sqrt(dist_sq + SOFTEN)


def matmul_hi(left, right):
    return jnp.dot(
        left, right, precision=lax.Precision.HIGHEST, preferred_element_type=jnp.float32
    )


def inner_cols(left, right):
    return lax.dot_general(
        left,
        right,
        (((0,), (0,)), ((), ())),
        precision=lax.Precision.HIGHEST,
        preferred_element_type=jnp.float32,
    )


def pack_plan(width, devices):
    tiles = width // LANES
    gram_rows = tiles * (tiles + 1) // 2 * LANES
    cross_rows = tiles * width
    need = gram_rows + cross_rows + SUB
    unit = SUB * devices * STREAMS
    total = -(-need // unit) * unit
    return tiles, gram_rows, cross_rows, total


def gram_slots(tiles):
    return [(i, j) for i in range(tiles) for j in range(i, tiles)]


def bit_orders(n_row, n_col):
    col_bits = [("col", b) for b in range(n_col.bit_length() - 1)]
    row_bits = [("row", b) for b in range(n_row.bit_length() - 1)]
    core, side = col_bits[:1], col_bits[1:]
    first = core + side + row_bits
    second = core + row_bits[:1] + side + row_bits[1:]
    return first, second


def reduce_kernel(
    n_row, n_col, gram_ref, cross_ref, self_ref, out_ref, buf, land, full, rs_send, rs_recv, ag_send, ag_recv
):
    width = gram_ref.shape[0]
    tiles, gram_rows, cross_rows, total = pack_plan(width, n_row * n_col)
    place = {"row": lax.axis_index("row"), "col": lax.axis_index("col")}

    def bit_of(step):
        axis, b = step
        return place[axis] // (1 << b) % 2

    def partner_of(step):
        axis, b = step
        other = place[axis] + (1 - 2 * bit_of(step)) * (1 << b)
        if axis == "row":
            return (other, place["col"])
        return (place["row"], other)

    orders = bit_orders(n_row, n_col)
    barrier = pltpu.get_barrier_semaphore()
    for step in orders[0]:
        pl.semaphore_signal(barrier, inc=1, device_id=partner_of(step), device_id_type=MESH)

    for slot, (i, j) in enumerate(gram_slots(tiles)):
        buf[slot * LANES : (slot + 1) * LANES, :] = gram_ref[
            i * LANES : (i + 1) * LANES, j * LANES : (j + 1) * LANES
        ]
    for j in range(tiles):
        at = gram_rows + j * width
        buf[at : at + width, :] = cross_ref[:, j * LANES : (j + 1) * LANES]
    at = gram_rows + cross_rows
    buf[at:total, :] = jnp.zeros((total - at, LANES), jnp.float32)
    for j in range(tiles):
        buf[at + j : at + j + 1, :] = self_ref[:, j * LANES : (j + 1) * LANES]

    pl.semaphore_wait(barrier, len(orders[0]))

    share = total // STREAMS
    steps = len(orders[0])
    starts = [s * share for s in range(STREAMS)]
    history = []
    land_at = 0
    size = share
    for t in range(steps):
        half = size // 2
        copies = []
        keeps = []
        for s in range(STREAMS):
            step = orders[s][t]
            bit = bit_of(step)
            keep = pl.multiple_of(starts[s] + bit * half, SUB)
            give = pl.multiple_of(starts[s] + (1 - bit) * half, SUB)
            landing = land.at[pl.ds(s * share + land_at, half), :]
            copy = pltpu.make_async_remote_copy(
                src_ref=buf.at[pl.ds(give, half), :],
                dst_ref=landing,
                send_sem=rs_send.at[s, t],
                recv_sem=rs_recv.at[s, t],
                device_id=partner_of(step),
                device_id_type=MESH,
            )
            copy.start()
            copies.append(copy)
            keeps.append(keep)
        for s in range(STREAMS):
            copies[s].wait()
            here = pl.ds(keeps[s], half)
            buf[here, :] = buf[here, :] + land[s * share + land_at : s * share + land_at + half, :]
        history.append(keeps)
        starts = keeps
        land_at += half
        size = half
    for s in range(STREAMS):
        here = pl.ds(starts[s], size)
        full[here, :] = buf[here, :]
    for t in reversed(range(steps)):
        copies = []
        for s in range(STREAMS):
            here = pl.ds(history[t][s], size)
            copy = pltpu.make_async_remote_copy(
                src_ref=full.at[here, :],
                dst_ref=full.at[here, :],
                send_sem=ag_send.at[s, t],
                recv_sem=ag_recv.at[s, t],
                device_id=partner_of(orders[s][t]),
                device_id_type=MESH,
            )
            copy.start()
            copies.append(copy)
        for s in range(STREAMS):
            copies[s].wait()
        size = size * 2
    out_ref[...] = full[...]


def global_sum(gram_mat, cross_mat, self_squares):
    n_row, n_col = lax.axis_size("row"), lax.axis_size("col")
    width = gram_mat.shape[0]
    total = pack_plan(width, n_row * n_col)[-1]
    steps = len(bit_orders(n_row, n_col)[0])
    vmem = pl.BlockSpec(memory_space=pltpu.VMEM)
    return pl.pallas_call(
        functools.partial(reduce_kernel, n_row, n_col),
        out_shape=jax.ShapeDtypeStruct((total, LANES), jnp.float32),
        in_specs=[vmem] * 3,
        out_specs=vmem,
        scratch_shapes=[
            pltpu.VMEM((total, LANES), jnp.float32),
            pltpu.VMEM((total, LANES), jnp.float32),
            pltpu.VMEM((total, LANES), jnp.float32),
            pltpu.SemaphoreType.DMA((STREAMS, steps)),
            pltpu.SemaphoreType.DMA((STREAMS, steps)),
            pltpu.SemaphoreType.DMA((STREAMS, steps)),
            pltpu.SemaphoreType.DMA((STREAMS, steps)),
        ],
        compiler_params=pltpu.CompilerParams(collective_id=1, has_side_effects=True),
        name="sum_all",
    )(gram_mat, cross_mat, self_squares)


def invert_tile(tile):
    size = tile.shape[0]
    lane = lax.broadcasted_iota(jnp.int32, (SUB, size), 1)
    sub = lax.broadcasted_iota(jnp.int32, (SUB, size), 0)

    def panel(_, mat):
        top, rest = mat[:SUB], mat[SUB:]
        top_cols = [jnp.broadcast_to(top[:, m : m + 1], (SUB, size)) for m in range(SUB)]
        top = jnp.where(lane < SUB, 0.0, top)
        for i in range(SUB):
            pivot = jnp.broadcast_to(top_cols[i][i : i + 1], (SUB, size))
            inv = 1.0 / pivot
            own = sub == i
            factor = jnp.where(own, 0.0, top_cols[i])
            row = jnp.broadcast_to(top[i : i + 1], (SUB, size)) * inv
            row = jnp.where(lane == i, inv, row)
            top = jnp.where(own, row, top - factor * row)
            for m in range(i + 1, SUB):
                entry = jnp.broadcast_to(top_cols[m][i : i + 1], (SUB, size)) * inv
                top_cols[m] = jnp.where(own, entry, top_cols[m] - factor * entry)
        lane_rest = lax.broadcasted_iota(jnp.int32, rest.shape, 1)
        fresh = jnp.where(lane_rest < SUB, 0.0, rest)
        for m in range(SUB):
            fresh = fresh - jnp.broadcast_to(rest[:, m : m + 1], rest.shape) * top[m : m + 1]
        mat = jnp.concatenate([fresh, top], axis=0)
        return pltpu.roll(mat, size - SUB, 1)

    return lax.fori_loop(0, size // SUB, panel, tile)


def solve_kernel(points_total, packed_ref, image_ref, res_ref, new_ref, norm_ref, g_ref, c_ref):
    width = c_ref.shape[0]
    tiles = width // LANES
    gram_rows = tiles * (tiles + 1) // 2 * LANES
    for slot, (i, j) in enumerate(gram_slots(tiles)):
        g_ref[i * LANES : (i + 1) * LANES, j * LANES : (j + 1) * LANES] = packed_ref[
            slot * LANES : (slot + 1) * LANES, :
        ]
    for j in range(tiles):
        at = gram_rows + j * width
        c_ref[:, j * LANES : (j + 1) * LANES] = packed_ref[at : at + width, :]

    for k in range(tiles):
        lo, hi = k * LANES, (k + 1) * LANES
        inverse = invert_tile(g_ref[lo:hi, lo:hi])
        if hi < width:
            link = g_ref[lo:hi, hi:]
            right = matmul_hi(inverse, link)
            for i in range(k + 1, tiles):
                a, b = i * LANES, (i + 1) * LANES
                g_ref[a:b, a:] = g_ref[a:b, a:] - inner_cols(
                    link[:, a - hi : b - hi], right[:, a - hi :]
                )
            g_ref[lo:hi, hi:] = right
            mid = matmul_hi(inverse, c_ref[lo:hi, :])
            c_ref[lo:hi, :] = mid
            c_ref[hi:, :] = c_ref[hi:, :] - inner_cols(link, mid)
        else:
            c_ref[lo:hi, :] = matmul_hi(inverse, c_ref[lo:hi, :])
    for k in reversed(range(tiles - 1)):
        lo, hi = k * LANES, (k + 1) * LANES
        c_ref[lo:hi, :] = c_ref[lo:hi, :] - matmul_hi(g_ref[lo:hi, hi:], c_ref[hi:, :])

    new_ref[...] = res_ref[...] - matmul_hi(image_ref[...], c_ref[...])
    for j in range(tiles):
        at = gram_rows + j * width
        cols = slice(j * LANES, (j + 1) * LANES)
        explained = jnp.sum(c_ref[:, cols] * packed_ref[at : at + width, :], axis=0, keepdims=True)
        here = gram_rows + tiles * width + j
        left = packed_ref[here : here + 1, :] - explained
        norm_ref[:, cols] = jnp.sqrt(jnp.maximum(left, 0.0) / points_total)


def solve_step(packed, image, residual_in, points_total):
    width = residual_in.shape[1]
    vmem = pl.BlockSpec(memory_space=pltpu.VMEM)
    new_residual, norms = pl.pallas_call(
        functools.partial(solve_kernel, points_total),
        out_shape=(
            jax.ShapeDtypeStruct(residual_in.shape, jnp.float32),
            jax.ShapeDtypeStruct((1, width), jnp.float32),
        ),
        in_specs=[vmem] * 3,
        out_specs=(vmem, vmem),
        scratch_shapes=[
            pltpu.VMEM((width, width), jnp.float32),
            pltpu.VMEM((width, width), jnp.float32),
        ],
        name="solve_all",
    )(packed, image, residual_in)
    return new_residual, norms[0]


def shards(
    coords, residual_in, link_mask, compress, expand, level_gain, level_couple, partner_perm
):
    below_xyz, below_rhs = from_behind((coords, residual_in), ("row", "col"), 1)
    above_xyz, above_rhs = from_behind((coords, residual_in), ("row", "col"), -1)
    rank_width = compress.shape[1]
    coeffs = inner_cols(compress, residual_in)

    def mix_level(current, partner, level_at):
        taken_rows = partner_perm[0, level_at]
        picked = jnp.take(partner, taken_rows, axis=0)
        gain_col = level_gain[0, level_at * rank_width : (level_at + 1) * rank_width][:, None]
        couple = level_couple[:, level_at * rank_width : (level_at + 1) * rank_width]
        return gain_col * current + matmul_hi(couple, picked)

    row_top = lax.axis_size("row").bit_length() - 2
    for index_row in range(ROW_LEVELS):
        partner = from_partner(coeffs, "row", row_top - index_row)
        coeffs = mix_level(coeffs, partner, index_row)
    col_top = lax.axis_size("col").bit_length() - 2
    for index_col in range(COL_LEVELS):
        partner = from_partner(coeffs, "col", col_top - index_col)
        coeffs = mix_level(coeffs, partner, ROW_LEVELS + index_col)
    far_field = matmul_hi(expand, coeffs)
    weights = link_mask.astype(jnp.float32)
    near_scale = (3.0 * coords.shape[1]) ** (-0.5)
    near_field = matmul_hi(kernel_tile(coords, coords), residual_in)
    near_field = near_field + weights[0, 0] * matmul_hi(kernel_tile(coords, below_xyz), below_rhs)
    near_field = near_field + weights[0, 1] * matmul_hi(kernel_tile(coords, above_xyz), above_rhs)
    near_field = near_scale * near_field
    image = 2.0 * residual_in + near_field + far_field
    gram_mat = inner_cols(image, image)
    cross_mat = inner_cols(image, residual_in)
    points_total = coords.shape[1] * lax.axis_size("row") * lax.axis_size("col")
    self_squares = jnp.sum(residual_in * residual_in, axis=0)[None, :]
    packed = global_sum(gram_mat, cross_mat, self_squares)
    return solve_step(packed, image, residual_in, points_total)


def solution(mesh):
    return jax.shard_map(
        shards,
        mesh=mesh,
        in_specs=(
            P(None, ("row", "col")),
            P(("row", "col"), None),
            P(("row", "col"), None),
            P(("row", "col"), None),
            P(("row", "col"), None),
            P(("row", "col"), None),
            P(("row", "col"), None),
            P(("row", "col"), None, None),
        ),
        out_specs=(P(("row", "col"), None), P()),
        check_vma=False,
    )
```

profile of v0, /device:TPU:0, one launch (start us, length us, event | category | flops | bytes accessed | tf_op | source)
XLA Modules:
  0.0 180.4 jit_solution(5725650085680421064)
XLA Ops:
  0.6 0.0 copy-start
  0.6 1.4 collective-permute-start.2
  2.1 3.6 %collective-permute-start = (f32[3,128]{1,0:T(4,128)}, f32[3,128]{1,0:T(4,128)}, u32[]{:S(2)}, u32[]{:S(2)}) collective-permute-start(f32[3,128]{1,0:T(4,128)} %param.10), channel_id=1, source_target_pairs={{0,1},{1,2},{2,3},{3,4},{4,5},{5,6},{6,7},{7,8},{8,9},{9,10},{10,1... | collective-permute-start | bytes 4616 | tf_op jit(solution)/shard_map/ppermute | solution.py:25
  5.7 1.3 collective-permute-start.3
  7.0 5.3 %collective-permute-start.1 = (f32[128,512]{1,0:T(8,128)}, f32[128,512]{1,0:T(8,128)}, u32[]{:S(2)}, u32[]{:S(2)}) collective-permute-start(f32[128,512]{1,0:T(8,128)} %res_ref.1), channel_id=1, source_target_pairs={{0,1},{1,2},{2,3},{3,4},{4,5},{5,6},{6,7},{7,8},{8,9},{9,10},{10,1... | collective-permute-start | bytes 786440 | tf_op jit(solution)/shard_map/ppermute | solution.py:25
  12.2 0.0 copy-done
  12.3 1.6 fusion.116
  13.8 5.7 %collective-permute-start.4 = (f32[256,512]{1,0:T(8,128)S(1)}, f32[256,512]{1,0:T(8,128)S(1)}, u32[]{:S(2)}, u32[]{:S(2)}) collective-permute-start(f32[256,512]{1,0:T(8,128)S(1)} %fusion.116), channel_id=1, source_target_pairs={{0,16},{16,0},{8,24},{24,8},{1,17},{17,1},{9,25},{25,9},{2,18},{18... | collective-permute-start | bytes 1572872 | tf_op jit(solution)/shard_map/ppermute | solution.py:35
  19.5 1.6 multiply_reduce_fusion
  21.1 0.7 fusion.114
  21.8 0.7 convert_element_type.3
  22.5 0.7 fusion.115
  23.1 0.6 compare_and_fusion.2
  23.7 0.6 compare_and_fusion
  24.3 0.5 compare_and_fusion.3
  24.9 0.0 copy-done.6
  24.9 1.4 fusion.113
  26.2 16.7 %collective-permute-done.4 = f32[256,512]{1,0:T(8,128)S(1)} collective-permute-done((f32[256,512]{1,0:T(8,128)S(1)}, f32[256,512]{1,0:T(8,128)S(1)}, u32[]{:S(2)}, u32[]{:S(2)}) %collective-permute-start.4) | collective-permute-done | bytes 524320 | tf_op jit(solution)/shard_map/ppermute | solution.py:35
  42.9 1.0 gather_fusion
  43.9 0.0 copy-done.3
  43.9 0.7 fusion
  44.7 0.1 collective-permute-start.5
  44.8 0.6 compare_select_fusion.2
  45.3 0.6 compare_select_fusion
  45.9 10.8 %collective-permute-done.5 = f32[256,512]{1,0:T(8,128)S(1)} collective-permute-done((f32[256,512]{1,0:T(8,128)S(1)}, f32[256,512]{1,0:T(8,128)S(1)}, u32[]{:S(2)}, u32[]{:S(2)}) %collective-permute-start.5) | collective-permute-done | bytes 524320 | tf_op jit(solution)/shard_map/ppermute | solution.py:35
  56.7 1.0 gather_fusion.1
  57.7 0.0 copy-start.13
  57.7 0.0 copy-start.1
  57.7 1.5 multiply_add_fusion.2
  59.2 0.5 collective-permute-start.6
  59.7 0.6 pad_clamp_fusion.2
  60.3 0.0 copy-done.1
  60.3 0.7 fusion.63
  61.0 9.4 %collective-permute-done.6 = f32[256,512]{1,0:T(8,128)S(1)} collective-permute-done((f32[256,512]{1,0:T(8,128)S(1)}, f32[256,512]{1,0:T(8,128)S(1)}, u32[]{:S(2)}, u32[]{:S(2)}) %collective-permute-start.6) | collective-permute-done | bytes 524320 | tf_op jit(solution)/shard_map/ppermute | solution.py:35
  70.3 1.1 gather_fusion.2
  71.5 1.4 multiply_add_fusion.1
  72.9 4.6 %collective-permute-start.7 = (f32[256,512]{1,0:T(8,128)S(1)}, f32[256,512]{1,0:T(8,128)S(1)}, u32[]{:S(2)}, u32[]{:S(2)}) collective-permute-start(f32[256,512]{1,0:T(8,128)S(1)} %multiply_add_fusion.1), channel_id=1, source_target_pairs={{0,2},{2,0},{1,3},{3,1},{4,6},{6,4},{5,7},{7,5},{8,10},{10,8},{9,1... | collective-permute-start | bytes 1572872 | tf_op jit(solution)/shard_map/ppermute | solution.py:35
  77.5 0.0 copy-done.7
  77.5 0.5 compare_and_fusion.1
  78.0 0.6 pad_clamp_fusion
  78.6 0.0 collective-permute-done.2
  78.6 1.4 slice_bitcast_fusion.2
  79.9 9.3 %collective-permute-done.7 = f32[256,512]{1,0:T(8,128)S(1)} collective-permute-done((f32[256,512]{1,0:T(8,128)S(1)}, f32[256,512]{1,0:T(8,128)S(1)}, u32[]{:S(2)}, u32[]{:S(2)}) %collective-permute-start.7) | collective-permute-done | bytes 524320 | tf_op jit(solution)/shard_map/ppermute | solution.py:35
  89.2 1.0 gather_fusion.3
  90.2 1.4 multiply_add_fusion
  91.7 0.1 collective-permute-start.8
  91.7 0.0 collective-permute-done
  91.8 0.8 slice_bitcast_fusion.5
  92.5 0.0 collective-permute-done.1
  92.5 2.3 %fusion.4 = f32[128,512]{1,0:T(8,128)S(1)} fusion(f32[128,512]{1,0:T(8,128)S(1)} %fusion.63, f32[128,512]{1,0:T(8,128)} %collective-permute-done.1, f32[]{:T(128)} %bitcast.3, f32[128]{0:T(128)S(1)} %get-tuple-element.21, f32[128]{0:T(128)S(1)} %get-tuple-element.22, f32[128]{0:T(128)S(1)} %get-tuple-element.20, f32[128]{0:T(128)S(1)} %get-tuple-element.24, ...), kind=kOutput, calls=%fused_computation.17 | convolution fusion | flops 100974592 | bytes 789508 | tf_op jit(solution)/shard_map/dot_general | solution.py:46
  94.9 0.0 collective-permute-done.3
  94.9 2.4 %fusion.5 = f32[128,512]{1,0:T(8,128)S(1)} fusion(f32[128,512]{1,0:T(8,128)S(1)} %fusion.4, f32[128,512]{1,0:T(8,128)} %collective-permute-done.3, f32[128,512]{1,0:T(8,128)S(1)} %copy-done.1, f32[]{:T(128)} %bitcast.7, f32[128]{0:T(128)S(1)} %copy-done.11, f32[128]{0:T(128)S(1)} %copy-done.12, f32[128]{0:T(128)S(1)} %copy-done.10, ...), kind=kOutput, calls=%fused_computation.18 | convolution fusion | flops 101171200 | bytes 1051652 | tf_op jit(solution)/shard_map/dot_general | solution.py:46
  97.3 0.0 collective-permute-done.8
  97.3 1.1 gather_fusion.4
  98.4 0.0 copy-done.14
  98.4 0.0 copy-start.4
  98.4 0.7 convolution_bitcast_fusion
  99.2 0.2 copy-done.4
  99.3 0.5 fusion.1.image_ref
  99.9 0.0 copy-start.2
  99.9 2.0 %fusion.118.cross_ref = f32[512,512]{1,0:T(8,128)} fusion(f32[128,512]{1,0:T(8,128)S(1)} %fusion.1.image_ref, f32[128,512]{1,0:T(8,128)S(1)} %copy-done.1), kind=kOutput, calls=%fused_computation.153 | convolution fusion | flops 402653184 | bytes 1572864 | tf_op jit(solution)/shard_map/dot_general | solution.py:52
  101.9 2.0 %fusion.117.gram_ref = f32[512,512]{1,0:T(8,128)} fusion(f32[128,512]{1,0:T(8,128)S(1)} %fusion.1.image_ref), kind=kOutput, calls=%fused_computation.152 | convolution fusion | flops 402653184 | bytes 1310720 | tf_op jit(solution)/shard_map/dot_general | solution.py:52
  103.9 47.4 %sum_all.1.packed_ref = f32[3584,128]{1,0:T(8,128)} custom-call(f32[512,512]{1,0:T(8,128)} %fusion.117.gram_ref, f32[512,512]{1,0:T(8,128)} %fusion.118.cross_ref, f32[1,512]{1,0:T(1,128)} %bitcast.64), custom_call_target="tpu_custom_call" | custom-call | tf_op jit(solution)/shard_map/sum_all/pallas_call | solution.py:185
  151.3 29.1 %solve_all.1 = (f32[128,512]{1,0:T(8,128)}, f32[1,512]{1,0:T(1,128)}) custom-call(f32[3584,128]{1,0:T(8,128)} %sum_all.1.packed_ref, f32[128,512]{1,0:T(8,128)} %copy-done.2, f32[128,512]{1,0:T(8,128)} %res_ref.1), custom_call_target="tpu_custom_call" | custom-call | tf_op jit(solution)/shard_map/solve_all/pallas_call | solution.py:280
  (26 shorter events, 0.1 us)
Async XLA Ops:
  0.6 11.6 %copy-start = (f32[128,256]{1,0:T(8,128)S(1)}, f32[128,256]{1,0:T(8,128)}, u32[]{:S(2)}) copy-start(f32[128,256]{1,0:T(8,128)} %param.13) | copy-start | bytes 393220
  0.6 77.9 %collective-permute-start.2 = (f32[3,128]{1,0:T(4,128)}, f32[3,128]{1,0:T(4,128)}, u32[]{:S(2)}, u32[]{:S(2)}) collective-permute-start(f32[3,128]{1,0:T(4,128)} %param.10), channel_id=1, source_target_pairs={{1,0},{2,1},{3,2},{4,3},{5,4},{6,5},{7,6},{8,7},{9,8},{10,9},{11,1... | collective-permute-start | bytes 4616 | tf_op jit(solution)/shard_map/ppermute | solution.py:25
  2.1 89.7 %collective-permute-start = (f32[3,128]{1,0:T(4,128)}, f32[3,128]{1,0:T(4,128)}, u32[]{:S(2)}, u32[]{:S(2)}) collective-permute-start(f32[3,128]{1,0:T(4,128)} %param.10), channel_id=1, source_target_pairs={{0,1},{1,2},{2,3},{3,4},{4,5},{5,6},{6,7},{7,8},{8,9},{9,10},{10,1... | collective-permute-start | bytes 4616 | tf_op jit(solution)/shard_map/ppermute | solution.py:25
  5.7 89.2 %collective-permute-start.3 = (f32[128,512]{1,0:T(8,128)}, f32[128,512]{1,0:T(8,128)}, u32[]{:S(2)}, u32[]{:S(2)}) collective-permute-start(f32[128,512]{1,0:T(8,128)} %res_ref.1), channel_id=1, source_target_pairs={{1,0},{2,1},{3,2},{4,3},{5,4},{6,5},{7,6},{8,7},{9,8},{10,9},{11,1... | collective-permute-start | bytes 786440 | tf_op jit(solution)/shard_map/ppermute | solution.py:25
  7.0 85.6 %collective-permute-start.1 = (f32[128,512]{1,0:T(8,128)}, f32[128,512]{1,0:T(8,128)}, u32[]{:S(2)}, u32[]{:S(2)}) collective-permute-start(f32[128,512]{1,0:T(8,128)} %res_ref.1), channel_id=1, source_target_pairs={{0,1},{1,2},{2,3},{3,4},{4,5},{5,6},{6,7},{7,8},{8,9},{9,10},{10,1... | collective-permute-start | bytes 786440 | tf_op jit(solution)/shard_map/ppermute | solution.py:25
  13.8 29.1 %collective-permute-start.4 = (f32[256,512]{1,0:T(8,128)S(1)}, f32[256,512]{1,0:T(8,128)S(1)}, u32[]{:S(2)}, u32[]{:S(2)}) collective-permute-start(f32[256,512]{1,0:T(8,128)S(1)} %fusion.116), channel_id=1, source_target_pairs={{0,16},{16,0},{8,24},{24,8},{1,17},{17,1},{9,25},{25,9},{2,18},{18... | collective-permute-start | bytes 1572872 | tf_op jit(solution)/shard_map/ppermute | solution.py:35
  21.8 3.1 %copy-start.6 = (s32[1,1,256]{2,0,1:T(1,128)}, s32[1,1,256]{2,0,1:T(1,128)S(1)}, u32[]{:S(2)}) copy-start(s32[1,1,256]{2,0,1:T(1,128)S(1)} %get-tuple-element.16) | copy-start | bytes 3076
  26.2 17.7 %copy-start.3 = (f32[256,1280]{1,0:T(8,128)S(1)}, f32[256,1280]{1,0:T(8,128)}, u32[]{:S(2)}) copy-start(f32[256,1280]{1,0:T(8,128)} %param.16) | copy-start | bytes 3932164
  44.7 12.0 %collective-permute-start.5 = (f32[256,512]{1,0:T(8,128)S(1)}, f32[256,512]{1,0:T(8,128)S(1)}, u32[]{:S(2)}, u32[]{:S(2)}) collective-permute-start(f32[256,512]{1,0:T(8,128)S(1)} %fusion), channel_id=1, source_target_pairs={{0,8},{8,0},{16,24},{24,16},{1,9},{9,1},{17,25},{25,17},{2,10},{10... | collective-permute-start | bytes 1572872 | tf_op jit(solution)/shard_map/ppermute | solution.py:35
  57.7 2.0 %copy-start.9 = (s32[256]{0:T(256)S(1)}, s32[256]{0:T(256)}, u32[]{:S(2)}) copy-start(s32[256]{0:T(256)} %compare_select_fusion.2) | copy-start | bytes 3076
  57.7 2.6 %copy-start.13 = (f32[3,128]{1,0:T(4,128)S(1)}, f32[3,128]{1,0:T(4,128)}, u32[]{:S(2)}) copy-start(f32[3,128]{1,0:T(4,128)} %param.10) | copy-start | bytes 4612
  57.7 2.6 %copy-start.1 = (f32[128,512]{1,0:T(8,128)S(1)}, f32[128,512]{1,0:T(8,128)}, u32[]{:S(2)}) copy-start(f32[128,512]{1,0:T(8,128)} %res_ref.1) | copy-start | bytes 786436
  59.2 11.2 %collective-permute-start.6 = (f32[256,512]{1,0:T(8,128)S(1)}, f32[256,512]{1,0:T(8,128)S(1)}, u32[]{:S(2)}, u32[]{:S(2)}) collective-permute-start(f32[256,512]{1,0:T(8,128)S(1)} %multiply_add_fusion.2), channel_id=1, source_target_pairs={{0,4},{4,0},{1,5},{5,1},{2,6},{6,2},{3,7},{7,3},{8,12},{12,8},{9,1... | collective-permute-start | bytes 1572872 | tf_op jit(solution)/shard_map/ppermute | solution.py:35
  71.5 6.0 %copy-start.7 = (s32[1,1,256]{2,0,1:T(1,128)S(1)}, s32[1,1,256]{2,0,1:T(1,128)}, u32[]{:S(2)}) copy-start(s32[1,1,256]{2,0,1:T(1,128)} %copy-done.6) | copy-start | bytes 3076
  71.5 6.5 %copy-start.8 = (s32[256]{0:T(256)S(1)}, s32[256]{0:T(256)}, u32[]{:S(2)}) copy-start(s32[256]{0:T(256)} %compare_select_fusion) | copy-start | bytes 3076
  72.9 16.4 %collective-permute-start.7 = (f32[256,512]{1,0:T(8,128)S(1)}, f32[256,512]{1,0:T(8,128)S(1)}, u32[]{:S(2)}, u32[]{:S(2)}) collective-permute-start(f32[256,512]{1,0:T(8,128)S(1)} %multiply_add_fusion.1), channel_id=1, source_target_pairs={{0,2},{2,0},{1,3},{3,1},{4,6},{6,4},{5,7},{7,5},{8,10},{10,8},{9,1... | collective-permute-start | bytes 1572872 | tf_op jit(solution)/shard_map/ppermute | solution.py:35
  90.2 4.7 %copy-start.10 = (f32[128]{0:T(128)S(1)}, f32[128]{0:T(128)}, u32[]{:S(2)}) copy-start(f32[128]{0:T(128)} %get-tuple-element.17) | copy-start | bytes 1540
  90.2 4.7 %copy-start.11 = (f32[128]{0:T(128)S(1)}, f32[128]{0:T(128)}, u32[]{:S(2)}) copy-start(f32[128]{0:T(128)} %get-tuple-element.18) | copy-start | bytes 1540
  90.2 4.7 %copy-start.12 = (f32[128]{0:T(128)S(1)}, f32[128]{0:T(128)}, u32[]{:S(2)}) copy-start(f32[128]{0:T(128)} %get-tuple-element.19) | copy-start | bytes 1540
  91.7 5.6 %collective-permute-start.8 = (f32[256,512]{1,0:T(8,128)S(1)}, f32[256,512]{1,0:T(8,128)S(1)}, u32[]{:S(2)}, u32[]{:S(2)}) collective-permute-start(f32[256,512]{1,0:T(8,128)S(1)} %multiply_add_fusion), channel_id=1, source_target_pairs={{0,1},{1,0},{2,3},{3,2},{4,5},{5,4},{6,7},{7,6},{8,9},{9,8},{10,11... | collective-permute-start | bytes 1572872 | tf_op jit(solution)/shard_map/ppermute | solution.py:35
  97.3 1.1 copy-start.14
  98.4 0.9 copy-start.4
  98.4 0.9 copy-start.5
  99.9 4.0 %copy-start.2 = (f32[128,512]{1,0:T(8,128)}, f32[128,512]{1,0:T(8,128)S(1)}, u32[]{:S(2)}) copy-start(f32[128,512]{1,0:T(8,128)S(1)} %fusion.1.image_ref) | copy-start | bytes 786436
where the time goes:
time: 181 us; the launch traced here: 180 us
  Pallas kernels  76.5 us (42%)
  waiting for transfers between devices  46.1 us (25%)
  starting transfers between devices  22.5 us (12%)
  matrix products  17.3 us (10%)
  local copies, waits for them, and re-layouts  10.3 us (6%)
  other arithmetic  6.79 us (4%)
    pallas_call x1, Pallas kernels, global_sum(): pl.pallas_call(functools.partial(reduce_kernel, n_row, n_col), out_shape=...  47.4 us
    ppermute x5, waiting for transfers between devices, from_partner(): return lax.ppermute(block, axis, route)  46.1 us
    pallas_call x1, Pallas kernels, solve_step(): pl.pallas_call(functools.partial(solve_kernel, points_total), out_shape=(...  29.1 us
    dot_general x9, matrix products, matmul_hi(): jnp.dot(left, right, precision=lax.Precision.HIGHEST, preferred_element_t...  11.7 us
    ppermute x4, starting transfers between devices, from_behind(): return lax.ppermute(block, axis, route)  11.6 us
    ppermute x5, starting transfers between devices, from_partner(): return lax.ppermute(block, axis, route)  10.9 us
    dot_general x3, matrix products, inner_cols(): lax.dot_general(left, right, (((0,), (0,)), ((), ())), precision=lax.Prec...  5.6 us
    gather x5, local copies, waits for them, and re-layouts, mix_level(): picked = jnp.take(partner, taken_rows, axis=0)  5.13 us
  transfers between devices with their start and end apart: 9, of which 4 were waited for; matrix products, arithmetic and copies ran while one was open for 15% of the time, Pallas kernels for 0%

commit v1 on v0

--- a/solution.py
+++ b/solution.py
@@ -19,26 +19,10 @@
 MESH = pl.DeviceIdType.MESH
 
 
-def from_behind(block, axis, distance):
-    devices = range(lax.axis_size(axis))
-    route = [(i - distance, i) for i in devices if i - distance in devices]
-    return lax.ppermute(block, axis, route)
-
-
-def from_partner(block, axis, distance):
-    count = lax.axis_size(axis)
-    route = []
-    for low in range(count):
-        high = low | 1 << distance
-        if high != low and high < count:
-            route += [(low, high), (high, low)]
-    return lax.ppermute(block, axis, route)
-
-
-def kernel_tile(own_xyz, other_xyz):
-    dist_sq = (own_xyz[0][:, None] - other_xyz[0][None, :]) ** 2
-    dist_sq = dist_sq + (own_xyz[1][:, None] - other_xyz[1][None, :]) ** 2
-    dist_sq = dist_sq + (own_xyz[2][:, None] - other_xyz[2][None, :]) ** 2
+def kernel_tile(own_cols, other_rows):
+    dist_sq = (own_cols[:, 0:1] - other_rows[0:1, :]) ** 2
+    dist_sq = dist_sq + (own_cols[:, 1:2] - other_rows[1:2, :]) ** 2
+    dist_sq = dist_sq + (own_cols[:, 2:3] - other_rows[2:3, :]) ** 2
     return jnp.cos(WAVENUM * jnp.sqrt(dist_sq)) / jnp.sqrt(dist_sq + SOFTEN)
 
 
@@ -82,9 +66,9 @@
 
 
 def reduce_kernel(
-    n_row, n_col, gram_ref, cross_ref, self_ref, out_ref, buf, land, full, rs_send, rs_recv, ag_send, ag_recv
+    n_row, n_col, image_ref, res_ref, out_ref, buf, land, full, rs_send, rs_recv, ag_send, ag_recv
 ):
-    width = gram_ref.shape[0]
+    width = image_ref.shape[1]
     tiles, gram_rows, cross_rows, total = pack_plan(width, n_row * n_col)
     place = {"row": lax.axis_index("row"), "col": lax.axis_index("col")}
 
@@ -104,17 +88,23 @@
     for step in orders[0]:
         pl.semaphore_signal(barrier, inc=1, device_id=partner_of(step), device_id_type=MESH)
 
-    for slot, (i, j) in enumerate(gram_slots(tiles)):
-        buf[slot * LANES : (slot + 1) * LANES, :] = gram_ref[
-            i * LANES : (i + 1) * LANES, j * LANES : (j + 1) * LANES
-        ]
-    for j in range(tiles):
-        at = gram_rows + j * width
-        buf[at : at + width, :] = cross_ref[:, j * LANES : (j + 1) * LANES]
+    slot = 0
+    for i in range(tiles):
+        rows = inner_cols(image_ref[:, i * LANES : (i + 1) * LANES], image_ref[:, i * LANES :])
+        for j in range(tiles - i):
+            at = slot * LANES
+            buf[at : at + LANES, :] = rows[:, j * LANES : (j + 1) * LANES]
+            slot += 1
+    for i in range(tiles):
+        rows = inner_cols(image_ref[:, i * LANES : (i + 1) * LANES], res_ref[...])
+        for j in range(tiles):
+            at = gram_rows + j * width + i * LANES
+            buf[at : at + LANES, :] = rows[:, j * LANES : (j + 1) * LANES]
     at = gram_rows + cross_rows
     buf[at:total, :] = jnp.zeros((total - at, LANES), jnp.float32)
+    squares = jnp.sum(res_ref[...] * res_ref[...], axis=0, keepdims=True)
     for j in range(tiles):
-        buf[at + j : at + j + 1, :] = self_ref[:, j * LANES : (j + 1) * LANES]
+        buf[at + j : at + j + 1, :] = squares[:, j * LANES : (j + 1) * LANES]
 
     pl.semaphore_wait(barrier, len(orders[0]))
 
@@ -176,16 +166,16 @@
     out_ref[...] = full[...]
 
 
-def global_sum(gram_mat, cross_mat, self_squares):
+def global_sum(image, residual_in):
     n_row, n_col = lax.axis_size("row"), lax.axis_size("col")
-    width = gram_mat.shape[0]
+    width = image.shape[1]
     total = pack_plan(width, n_row * n_col)[-1]
     steps = len(bit_orders(n_row, n_col)[0])
     vmem = pl.BlockSpec(memory_space=pltpu.VMEM)
     return pl.pallas_call(
         functools.partial(reduce_kernel, n_row, n_col),
         out_shape=jax.ShapeDtypeStruct((total, LANES), jnp.float32),
-        in_specs=[vmem] * 3,
+        in_specs=[vmem] * 2,
         out_specs=vmem,
         scratch_shapes=[
             pltpu.VMEM((total, LANES), jnp.float32),
@@ -198,7 +188,7 @@
         ],
         compiler_params=pltpu.CompilerParams(collective_id=1, has_side_effects=True),
         name="sum_all",
-    )(gram_mat, cross_mat, self_squares)
+    )(image, residual_in)
 
 
 def invert_tile(tile):
@@ -294,42 +284,202 @@
     return new_residual, norms[0]
 
 
+def image_kernel(
+    n_row, n_col,
+    coords_ref, points_ref, res_ref, mask_ref, comp_ref, exp_ref, gain_ref, couple_ref, perm_ref,
+    image_ref,
+    mixed, gains, coef, land, land_res, land_comp, halo_res, halo_xyz,
+    comp_sems, res_sems, halo_sems, xyz_sems, level_sems,
+):
+    rank = comp_ref.shape[1]
+    width = res_ref.shape[1]
+    chunks = width // LANES
+    levels = ROW_LEVELS + COL_LEVELS
+    at_row, at_col = lax.axis_index("row"), lax.axis_index("col")
+    group = at_row * n_col + at_col
+    has_side = (group > 0, group < n_row * n_col - 1)
+
+    def partner_of(level):
+        if level < ROW_LEVELS:
+            bit = n_row.bit_length() - 2 - level
+            return (at_row + (1 - 2 * (at_row // (1 << bit) % 2)) * (1 << bit), at_col)
+        bit = n_col.bit_length() - 2 - (level - ROW_LEVELS)
+        return (at_row, at_col + (1 - 2 * (at_col // (1 << bit) % 2)) * (1 << bit))
+
+    def beside(side):
+        other = group + (2 * side - 1)
+        return (other // n_col, other % n_col)
+
+    def remote(src, dst, sems, where):
+        return pltpu.make_async_remote_copy(
+            src_ref=src,
+            dst_ref=dst,
+            send_sem=sems.at[0],
+            recv_sem=sems.at[1],
+            device_id=where,
+            device_id_type=MESH,
+        )
+
+    barrier = pltpu.get_barrier_semaphore()
+    for level in range(levels):
+        pl.semaphore_signal(barrier, inc=1, device_id=partner_of(level), device_id_type=MESH)
+    for side in range(2):
+        @pl.when(has_side[side])
+        def _():
+            pl.semaphore_signal(barrier, inc=1, device_id=beside(side), device_id_type=MESH)
+    sides = jnp.minimum(group, 1) + jnp.minimum(n_row * n_col - 1 - group, 1)
+    pl.semaphore_wait(barrier, levels + sides)
+
+    def cols(k):
+        return pl.ds(k * LANES, LANES)
+
+    comp_copy = remote(comp_ref, land_comp, comp_sems, partner_of(0))
+    comp_copy.start()
+    res_copies = []
+    for k in range(chunks):
+        copy = remote(res_ref.at[:, cols(k)], land_res.at[k], res_sems.at[k], partner_of(0))
+        copy.start()
+        res_copies.append(copy)
+    halo_copies = [
+        (
+            remote(coords_ref, halo_xyz.at[1 - side], xyz_sems.at[side], beside(side)),
+            remote(res_ref, halo_res.at[1 - side], halo_sems.at[side], beside(side)),
+        )
+        for side in range(2)
+    ]
+    halo_waits = [
+        (
+            remote(coords_ref, halo_xyz.at[side], xyz_sems.at[1 - side], beside(side)),
+            remote(res_ref, halo_res.at[side], halo_sems.at[1 - side], beside(side)),
+        )
+        for side in range(2)
+    ]
+    for side in range(2):
+        @pl.when(has_side[side])
+        def _():
+            halo_copies[side][0].start()
+            halo_copies[side][1].start()
+
+        @pl.when(jnp.logical_not(has_side[side]))
+        def _():
+            halo_xyz[side] = jnp.zeros(halo_xyz.shape[1:], jnp.float32)
+            halo_res[side] = jnp.zeros(halo_res.shape[1:], jnp.float32)
+
+    down = lax.broadcasted_iota(jnp.int32, (rank, rank), 0)
+    across = lax.broadcasted_iota(jnp.int32, (rank, rank), 1)
+    for level in range(levels):
+        here = slice(level * rank, (level + 1) * rank)
+        taken = jnp.where(down == perm_ref[0, level : level + 1, :], 1.0, 0.0)
+        mixed[level] = lax.dot_general(
+            couple_ref[:, here],
+            taken,
+            (((1,), (1,)), ((), ())),
+            precision=lax.Precision.HIGHEST,
+            preferred_element_type=jnp.float32,
+        )
+        spread = jnp.where(down == across, gain_ref[:, here], 0.0)
+        gains[level] = jnp.broadcast_to(jnp.sum(spread, axis=1, keepdims=True), (rank, LANES))
+
+    own = inner_cols(comp_ref[...], res_ref[...])
+    near_scale = (3.0 * res_ref.shape[0]) ** (-0.5)
+    own_tile = near_scale * kernel_tile(points_ref[...], coords_ref[...])
+    image_ref[...] = 2.0 * res_ref[...] + matmul_hi(own_tile, res_ref[...])
+
+    comp_copy.wait()
+    first = lax.dot_general(
+        mixed[0],
+        land_comp[...],
+        (((1,), (1,)), ((), ())),
+        precision=lax.Precision.HIGHEST,
+        preferred_element_type=jnp.float32,
+    )
+
+    copies = {}
+
+    def step(level, k):
+        if level == 0:
+            res_copies[k].wait()
+            fresh = gains[0] * own[:, k * LANES : (k + 1) * LANES] + matmul_hi(first, land_res[k])
+        else:
+            copies[level, k].wait()
+            fresh = gains[level] * coef[level - 1, k] + matmul_hi(mixed[level], land[level - 1, k])
+        if level == levels - 1:
+            image_ref[:, cols(k)] = image_ref[:, cols(k)] + matmul_hi(exp_ref[...], fresh)
+            return
+        coef[level, k] = fresh
+        copy = remote(coef.at[level, k], land.at[level, k], level_sems.at[level, k], partner_of(level + 1))
+        copy.start()
+        copies[level + 1, k] = copy
+
+    def near_side(side):
+        @pl.when(has_side[side])
+        def _():
+            for copy in halo_copies[side]:
+                copy.wait_send()
+            for copy in halo_waits[side]:
+                copy.wait_recv()
+
+        keep = mask_ref[0:1, side : side + 1].astype(jnp.float32) * near_scale
+        tile = keep * kernel_tile(points_ref[...], halo_xyz[side])
+        image_ref[...] = image_ref[...] + matmul_hi(tile, halo_res[side])
+
+    for wave in range(levels + chunks - 1):
+        for level in reversed(range(levels)):
+            if 0 <= wave - level < chunks:
+                step(level, wave - level)
+        if wave == chunks - 1:
+            near_side(0)
+        if wave == chunks:
+            near_side(1)
+
+
+def local_image(
+    coords, residual_in, link_mask, compress, expand, level_gain, level_couple, partner_perm
+):
+    n_row, n_col = lax.axis_size("row"), lax.axis_size("col")
+    points, width = residual_in.shape
+    rank = compress.shape[1]
+    chunks = width // LANES
+    levels = ROW_LEVELS + COL_LEVELS
+    vmem = pl.BlockSpec(memory_space=pltpu.VMEM)
+    dma = pltpu.SemaphoreType.DMA
+    f32 = jnp.float32
+    return pl.pallas_call(
+        functools.partial(image_kernel, n_row, n_col),
+        out_shape=jax.ShapeDtypeStruct((points, width), f32),
+        in_specs=[vmem] * 9,
+        out_specs=vmem,
+        scratch_shapes=[
+            pltpu.VMEM((levels, rank, rank), f32),
+            pltpu.VMEM((levels, rank, LANES), f32),
+            pltpu.VMEM((levels - 1, chunks, rank, LANES), f32),
+            pltpu.VMEM((levels - 1, chunks, rank, LANES), f32),
+            pltpu.VMEM((chunks, points, LANES), f32),
+            pltpu.VMEM((points, rank), f32),
+            pltpu.VMEM((2, points, width), f32),
+            pltpu.VMEM((2, coords.shape[0], points), f32),
+            dma((2,)),
+            dma((chunks, 2)),
+            dma((2, 2)),
+            dma((2, 2)),
+            dma((levels - 1, chunks, 2)),
+        ],
+        compiler_params=pltpu.CompilerParams(collective_id=2, has_side_effects=True),
+        name="image_all",
+    )(
+        coords, coords.T, residual_in, link_mask, compress, expand, level_gain, level_couple,
+        partner_perm,
+    )
+
+
 def shards(
     coords, residual_in, link_mask, compress, expand, level_gain, level_couple, partner_perm
 ):
-    below_xyz, below_rhs = from_behind((coords, residual_in), ("row", "col"), 1)
-    above_xyz, above_rhs = from_behind((coords, residual_in), ("row", "col"), -1)
-    rank_width = compress.shape[1]
-    coeffs = inner_cols(compress, residual_in)
-
-    def mix_level(current, partner, level_at):
-        taken_rows = partner_perm[0, level_at]
-        picked = jnp.take(partner, taken_rows, axis=0)
-        gain_col = level_gain[0, level_at * rank_width : (level_at + 1) * rank_width][:, None]
-        couple = level_couple[:, level_at * rank_width : (level_at + 1) * rank_width]
-        return gain_col * current + matmul_hi(couple, picked)
-
-    row_top = lax.axis_size("row").bit_length() - 2
-    for index_row in range(ROW_LEVELS):
-        partner = from_partner(coeffs, "row", row_top - index_row)
-        coeffs = mix_level(coeffs, partner, index_row)
-    col_top = lax.axis_size("col").bit_length() - 2
-    for index_col in range(COL_LEVELS):
-        partner = from_partner(coeffs, "col", col_top - index_col)
-        coeffs = mix_level(coeffs, partner, ROW_LEVELS + index_col)
-    far_field = matmul_hi(expand, coeffs)
-    weights = link_mask.astype(jnp.float32)
-    near_scale = (3.0 * coords.shape[1]) ** (-0.5)
-    near_field = matmul_hi(kernel_tile(coords, coords), residual_in)
-    near_field = near_field + weights[0, 0] * matmul_hi(kernel_tile(coords, below_xyz), below_rhs)
-    near_field = near_field + weights[0, 1] * matmul_hi(kernel_tile(coords, above_xyz), above_rhs)
-    near_field = near_scale * near_field
-    image = 2.0 * residual_in + near_field + far_field
-    gram_mat = inner_cols(image, image)
-    cross_mat = inner_cols(image, residual_in)
+    image = local_image(
+        coords, residual_in, link_mask, compress, expand, level_gain, level_couple, partner_perm
+    )
     points_total = coords.shape[1] * lax.axis_size("row") * lax.axis_size("col")
-    self_squares = jnp.sum(residual_in * residual_in, axis=0)[None, :]
-    packed = global_sum(gram_mat, cross_mat, self_squares)
+    packed = global_sum(image, residual_in)
     return solve_step(packed, image, residual_in, points_total)
 
 

time: 181 us -> 133 us (0.73)
  Pallas kernels: 76.5 us -> 130 us
  waiting for transfers between devices: 46.1 us -> 0 us
  starting transfers between devices: 22.5 us -> 0 us
  matrix products: 17.3 us -> 0 us
  local copies, waits for them, and re-layouts: 10.3 us -> 2.69 us
  other arithmetic: 6.79 us -> 0 us
    pallas_call x0 -> x1, Pallas kernels: none -> 55.3 us  [local_image(): pl.pallas_call(functools.partial(image_kernel, n_row, n_col), out_shape=j...]
    ppermute x9 -> x0, waiting for transfers between devices: 46.1 us -> none  [the longest x5 46.1 us: from_partner(): return lax.ppermute(block, axis, route)]
    ppermute x9 -> x0, starting transfers between devices: 22.5 us -> none  [the longest x4 11.6 us: from_behind(): return lax.ppermute(block, axis, route)]
    dot_general x12 -> x0, matrix products: 17.3 us -> none  [the longest x9 11.7 us: matmul_hi(): jnp.dot(left, right, precision=lax.Precision.HIGHEST, preferred_element_t...]
    gather x5 -> x0, local copies, waits for them, and re-layouts: 5.13 us -> none  [mix_level(): picked = jnp.take(partner, taken_rows, axis=0)]
    slice x3 -> x0, local copies, waits for them, and re-layouts: 2.75 us -> none  [the longest x1 1.35 us: mix_level(): level_gain[0, level_at * rank_width:(level_at + 1) * rank_width][:, None]]
    unnamed x30 -> x2, local copies, waits for them, and re-layouts: 0.22 us -> 2.69 us
    and x5 -> x0, other arithmetic: 2.18 us -> none  [mix_level(): picked = jnp.take(partner, taken_rows, axis=0)]
  transfers between devices with their start and end apart: 9 -> 0, of which waited for: 4 -> 0; matrix products, arithmetic and copies ran while one was open for 15% -> 0% of each run, Pallas kernels for 0% -> 0%
where the time goes in v1:
time: 133 us
  Pallas kernels  130 us (98%)
  local copies, waits for them, and re-layouts  2.69 us (2%)
    pallas_call x1, Pallas kernels, local_image(): pl.pallas_call(functools.partial(image_kernel, n_row, n_col), out_shape=j...  55.3 us
    pallas_call x1, Pallas kernels, global_sum(): pl.pallas_call(functools.partial(reduce_kernel, n_row, n_col), out_shape=...  45.5 us
    pallas_call x1, Pallas kernels, solve_step(): pl.pallas_call(functools.partial(solve_kernel, points_total), out_shape=(...  28.9 us
    unnamed x2, local copies, waits for them, and re-layouts  2.69 us

profile of v1, /device:TPU:0, one launch (start us, length us, event | category | flops | bytes accessed | tf_op | source)
XLA Modules:
  0.0 133.0 jit_solution(14740039846711586377)
XLA Ops:
  0.6 1.3 copy.11.perm_ref
  1.9 1.4 %copy.10 = f32[3,128]{0,1:T(8,128)} copy(f32[3,128]{1,0:T(4,128)} %coords_ref.1) | data formatting | bytes 3072 | tf_op args[0]
  3.3 55.3 %image_all.1.image_ref = f32[128,512]{1,0:T(8,128)} custom-call(f32[3,128]{1,0:T(4,128)} %coords_ref.1, f32[128,3]{1,0:T(8,128)} %bitcast.2, f32[128,512]{1,0:T(8,128)} %res_ref.5, s32[1,2]{1,0:T(1,128)} %mask_ref.1, f32[128,256]{1,0:T(8,128)} %comp_ref.1, f32[128,256]{1,0:T(8,128)} %exp_ref.1, f32[1,1280]{1,0:T(1,128)} %gain_ref.1, f32[256,1280]{1,0:T(8,128)} %couple_ref.1, ...), custom_call_target="tpu_custom_call" | custom-call | tf_op jit(solution)/shard_map/image_all/pallas_call | solution.py:447
  58.7 45.5 %sum_all.1.packed_ref = f32[3584,128]{1,0:T(8,128)} custom-call(f32[128,512]{1,0:T(8,128)} %image_all.1.image_ref, f32[128,512]{1,0:T(8,128)} %res_ref.5), custom_call_target="tpu_custom_call" | custom-call | tf_op jit(solution)/shard_map/sum_all/pallas_call | solution.py:175
  104.1 28.9 %solve_all.1 = (f32[128,512]{1,0:T(8,128)}, f32[1,512]{1,0:T(1,128)}) custom-call(f32[3584,128]{1,0:T(8,128)} %sum_all.1.packed_ref, f32[128,512]{1,0:T(8,128)} %image_all.1.image_ref, f32[128,512]{1,0:T(8,128)} %res_ref.5), custom_call_target="tpu_custom_call" | custom-call | tf_op jit(solution)/shard_map/solve_all/pallas_call | solution.py:270

commit v2 on v1

--- a/solution.py
+++ b/solution.py
@@ -15,7 +15,8 @@
 SOFTEN = 0.01
 LANES = 128
 SUB = 8
-STREAMS = 2
+GRAM_STREAMS = 3
+CROSS_STREAMS = 2
 MESH = pl.DeviceIdType.MESH
 
 
@@ -42,75 +43,39 @@
     )
 
 
-def pack_plan(width, devices):
-    tiles = width // LANES
-    gram_rows = tiles * (tiles + 1) // 2 * LANES
-    cross_rows = tiles * width
-    need = gram_rows + cross_rows + SUB
-    unit = SUB * devices * STREAMS
-    total = -(-need // unit) * unit
-    return tiles, gram_rows, cross_rows, total
+def padded(rows, devices, streams):
+    unit = SUB * devices * streams
+    return -(-rows // unit) * unit
 
 
 def gram_slots(tiles):
     return [(i, j) for i in range(tiles) for j in range(i, tiles)]
 
 
-def bit_orders(n_row, n_col):
+def stream_orders(n_row, n_col, streams):
     col_bits = [("col", b) for b in range(n_col.bit_length() - 1)]
     row_bits = [("row", b) for b in range(n_row.bit_length() - 1)]
-    core, side = col_bits[:1], col_bits[1:]
-    first = core + side + row_bits
-    second = core + row_bits[:1] + side + row_bits[1:]
-    return first, second
-
-
-def reduce_kernel(
-    n_row, n_col, image_ref, res_ref, out_ref, buf, land, full, rs_send, rs_recv, ag_send, ag_recv
-):
-    width = image_ref.shape[1]
-    tiles, gram_rows, cross_rows, total = pack_plan(width, n_row * n_col)
+    lead = col_bits[1:] + row_bits[:1]
+    tail = col_bits[:1] + row_bits[1:]
+    return [lead[s:] + lead[:s] + tail for s in range(streams)]
+
+
+def bit_of(step):
+    axis, b = step
+    return lax.axis_index(axis) // (1 << b) % 2
+
+
+def flipped(step):
+    axis, b = step
     place = {"row": lax.axis_index("row"), "col": lax.axis_index("col")}
-
-    def bit_of(step):
-        axis, b = step
-        return place[axis] // (1 << b) % 2
-
-    def partner_of(step):
-        axis, b = step
-        other = place[axis] + (1 - 2 * bit_of(step)) * (1 << b)
-        if axis == "row":
-            return (other, place["col"])
-        return (place["row"], other)
-
-    orders = bit_orders(n_row, n_col)
-    barrier = pltpu.get_barrier_semaphore()
-    for step in orders[0]:
-        pl.semaphore_signal(barrier, inc=1, device_id=partner_of(step), device_id_type=MESH)
-
-    slot = 0
-    for i in range(tiles):
-        rows = inner_cols(image_ref[:, i * LANES : (i + 1) * LANES], image_ref[:, i * LANES :])
-        for j in range(tiles - i):
-            at = slot * LANES
-            buf[at : at + LANES, :] = rows[:, j * LANES : (j + 1) * LANES]
-            slot += 1
-    for i in range(tiles):
-        rows = inner_cols(image_ref[:, i * LANES : (i + 1) * LANES], res_ref[...])
-        for j in range(tiles):
-            at = gram_rows + j * width + i * LANES
-            buf[at : at + LANES, :] = rows[:, j * LANES : (j + 1) * LANES]
-    at = gram_rows + cross_rows
-    buf[at:total, :] = jnp.zeros((total - at, LANES), jnp.float32)
-    squares = jnp.sum(res_ref[...] * res_ref[...], axis=0, keepdims=True)
-    for j in range(tiles):
-        buf[at + j : at + j + 1, :] = squares[:, j * LANES : (j + 1) * LANES]
-
-    pl.semaphore_wait(barrier, len(orders[0]))
-
-    share = total // STREAMS
-    steps = len(orders[0])
-    starts = [s * share for s in range(STREAMS)]
+    place[axis] = place[axis] + (1 - 2 * bit_of(step)) * (1 << b)
+    return (place["row"], place["col"])
+
+
+def sum_phases(orders, buf, land, full, rs_send, rs_recv, ag_send, ag_recv):
+    streams, steps = len(orders), len(orders[0])
+    share = buf.shape[0] // streams
+    starts = [s * share for s in range(streams)]
     history = []
     land_at = 0
     size = share
@@ -118,80 +83,55 @@
         half = size // 2
         copies = []
         keeps = []
-        for s in range(STREAMS):
+        for s in range(streams):
             step = orders[s][t]
             bit = bit_of(step)
-            keep = pl.multiple_of(starts[s] + bit * half, SUB)
+            keeps.append(pl.multiple_of(starts[s] + bit * half, SUB))
             give = pl.multiple_of(starts[s] + (1 - bit) * half, SUB)
-            landing = land.at[pl.ds(s * share + land_at, half), :]
             copy = pltpu.make_async_remote_copy(
                 src_ref=buf.at[pl.ds(give, half), :],
-                dst_ref=landing,
+                dst_ref=land.at[pl.ds(s * share + land_at, half), :],
                 send_sem=rs_send.at[s, t],
                 recv_sem=rs_recv.at[s, t],
-                device_id=partner_of(step),
+                device_id=flipped(step),
                 device_id_type=MESH,
             )
             copy.start()
             copies.append(copy)
-            keeps.append(keep)
-        for s in range(STREAMS):
+        yield
+        for s in range(streams):
             copies[s].wait()
             here = pl.ds(keeps[s], half)
-            buf[here, :] = buf[here, :] + land[s * share + land_at : s * share + land_at + half, :]
+            got = land[s * share + land_at : s * share + land_at + half, :]
+            if t == steps - 1:
+                full[here, :] = buf[here, :] + got
+            else:
+                buf[here, :] = buf[here, :] + got
         history.append(keeps)
         starts = keeps
         land_at += half
         size = half
-    for s in range(STREAMS):
-        here = pl.ds(starts[s], size)
-        full[here, :] = buf[here, :]
     for t in reversed(range(steps)):
         copies = []
-        for s in range(STREAMS):
-            here = pl.ds(history[t][s], size)
+        for s in range(streams):
+            here = full.at[pl.ds(history[t][s], size), :]
             copy = pltpu.make_async_remote_copy(
-                src_ref=full.at[here, :],
-                dst_ref=full.at[here, :],
+                src_ref=here,
+                dst_ref=here,
                 send_sem=ag_send.at[s, t],
                 recv_sem=ag_recv.at[s, t],
-                device_id=partner_of(orders[s][t]),
+                device_id=flipped(orders[s][t]),
                 device_id_type=MESH,
             )
             copy.start()
             copies.append(copy)
-        for s in range(STREAMS):
-            copies[s].wait()
+        yield
+        for copy in copies:
+            copy.wait()
         size = size * 2
-    out_ref[...] = full[...]
-
-
-def global_sum(image, residual_in):
-    n_row, n_col = lax.axis_size("row"), lax.axis_size("col")
-    width = image.shape[1]
-    total = pack_plan(width, n_row * n_col)[-1]
-    steps = len(bit_orders(n_row, n_col)[0])
-    vmem = pl.BlockSpec(memory_space=pltpu.VMEM)
-    return pl.pallas_call(
-        functools.partial(reduce_kernel, n_row, n_col),
-        out_shape=jax.ShapeDtypeStruct((total, LANES), jnp.float32),
-        in_specs=[vmem] * 2,
-        out_specs=vmem,
-        scratch_shapes=[
-            pltpu.VMEM((total, LANES), jnp.float32),
-            pltpu.VMEM((total, LANES), jnp.float32),
-            pltpu.VMEM((total, LANES), jnp.float32),
-            pltpu.SemaphoreType.DMA((STREAMS, steps)),
-            pltpu.SemaphoreType.DMA((STREAMS, steps)),
-            pltpu.SemaphoreType.DMA((STREAMS, steps)),
-            pltpu.SemaphoreType.DMA((STREAMS, steps)),
-        ],
-        compiler_params=pltpu.CompilerParams(collective_id=1, has_side_effects=True),
-        name="sum_all",
-    )(image, residual_in)
-
-
-def invert_tile(tile):
+
+
+def invert_panels(tile, count):
     size = tile.shape[0]
     lane = lax.broadcasted_iota(jnp.int32, (SUB, size), 1)
     sub = lax.broadcasted_iota(jnp.int32, (SUB, size), 0)
@@ -218,24 +158,64 @@
         mat = jnp.concatenate([fresh, top], axis=0)
         return pltpu.roll(mat, size - SUB, 1)
 
-    return lax.fori_loop(0, size // SUB, panel, tile)
-
-
-def solve_kernel(points_total, packed_ref, image_ref, res_ref, new_ref, norm_ref, g_ref, c_ref):
-    width = c_ref.shape[0]
+    return lax.fori_loop(0, count, panel, tile)
+
+
+def finish_kernel(
+    n_row, n_col, image_ref, res_ref, new_ref, norm_ref,
+    g_buf, g_land, g_full, c_buf, c_land, c_full, g_ref, c_ref, inv_ref, *sems
+):
+    width = image_ref.shape[1]
     tiles = width // LANES
+    points_total = image_ref.shape[0] * n_row * n_col
     gram_rows = tiles * (tiles + 1) // 2 * LANES
+    g_orders = stream_orders(n_row, n_col, GRAM_STREAMS)
+    c_orders = stream_orders(n_row, n_col, CROSS_STREAMS)
+
+    barrier = pltpu.get_barrier_semaphore()
+    for step in g_orders[0]:
+        pl.semaphore_signal(barrier, inc=1, device_id=flipped(step), device_id_type=MESH)
+
+    slot = 0
+    for i in range(tiles):
+        rows = inner_cols(image_ref[:, i * LANES : (i + 1) * LANES], image_ref[:, i * LANES :])
+        for j in range(tiles - i):
+            at = slot * LANES
+            g_buf[at : at + LANES, :] = rows[:, j * LANES : (j + 1) * LANES]
+            slot += 1
+    g_buf[gram_rows:, :] = jnp.zeros((g_buf.shape[0] - gram_rows, LANES), jnp.float32)
+    squares = jnp.sum(res_ref[...] * res_ref[...], axis=0, keepdims=True)
+    for j in range(tiles):
+        g_buf[gram_rows + j : gram_rows + j + 1, :] = squares[:, j * LANES : (j + 1) * LANES]
+
+    pl.semaphore_wait(barrier, len(g_orders[0]))
+    gram_sum = sum_phases(g_orders, g_buf, g_land, g_full, *sems[:4])
+    next(gram_sum)
+    for i in range(tiles):
+        rows = inner_cols(image_ref[:, i * LANES : (i + 1) * LANES], res_ref[...])
+        for j in range(tiles):
+            at = j * width + i * LANES
+            c_buf[at : at + LANES, :] = rows[:, j * LANES : (j + 1) * LANES]
+    spare = c_buf.shape[0] - tiles * width
+    if spare:
+        c_buf[tiles * width :, :] = jnp.zeros((spare, LANES), jnp.float32)
+    for _ in gram_sum:
+        pass
+    cross_sum = sum_phases(c_orders, c_buf, c_land, c_full, *sems[4:])
+    next(cross_sum)
+
     for slot, (i, j) in enumerate(gram_slots(tiles)):
-        g_ref[i * LANES : (i + 1) * LANES, j * LANES : (j + 1) * LANES] = packed_ref[
+        g_ref[i * LANES : (i + 1) * LANES, j * LANES : (j + 1) * LANES] = g_full[
             slot * LANES : (slot + 1) * LANES, :
         ]
-    for j in range(tiles):
-        at = gram_rows + j * width
-        c_ref[:, j * LANES : (j + 1) * LANES] = packed_ref[at : at + width, :]
-
+    panels = LANES // SUB
     for k in range(tiles):
         lo, hi = k * LANES, (k + 1) * LANES
-        inverse = invert_tile(g_ref[lo:hi, lo:hi])
+        inverse = invert_panels(g_ref[lo:hi, lo:hi], panels // 2)
+        next(cross_sum, None)
+        inverse = invert_panels(inverse, panels - panels // 2)
+        inv_ref[lo:hi, :] = inverse
+        next(cross_sum, None)
         if hi < width:
             link = g_ref[lo:hi, hi:]
             right = matmul_hi(inverse, link)
@@ -245,42 +225,56 @@
                     link[:, a - hi : b - hi], right[:, a - hi :]
                 )
             g_ref[lo:hi, hi:] = right
-            mid = matmul_hi(inverse, c_ref[lo:hi, :])
-            c_ref[lo:hi, :] = mid
-            c_ref[hi:, :] = c_ref[hi:, :] - inner_cols(link, mid)
-        else:
-            c_ref[lo:hi, :] = matmul_hi(inverse, c_ref[lo:hi, :])
+            next(cross_sum, None)
+    for _ in cross_sum:
+        pass
+
+    for j in range(tiles):
+        c_ref[:, j * LANES : (j + 1) * LANES] = c_full[j * width : (j + 1) * width, :]
+    for k in range(tiles):
+        lo, hi = k * LANES, (k + 1) * LANES
+        part = c_ref[lo:hi, :]
+        c_ref[lo:hi, :] = matmul_hi(inv_ref[lo:hi, :], part)
+        if hi < width:
+            c_ref[hi:, :] = c_ref[hi:, :] - inner_cols(g_ref[lo:hi, hi:], part)
     for k in reversed(range(tiles - 1)):
         lo, hi = k * LANES, (k + 1) * LANES
         c_ref[lo:hi, :] = c_ref[lo:hi, :] - matmul_hi(g_ref[lo:hi, hi:], c_ref[hi:, :])
 
     new_ref[...] = res_ref[...] - matmul_hi(image_ref[...], c_ref[...])
     for j in range(tiles):
-        at = gram_rows + j * width
         cols = slice(j * LANES, (j + 1) * LANES)
-        explained = jnp.sum(c_ref[:, cols] * packed_ref[at : at + width, :], axis=0, keepdims=True)
-        here = gram_rows + tiles * width + j
-        left = packed_ref[here : here + 1, :] - explained
+        cross = c_full[j * width : (j + 1) * width, :]
+        explained = jnp.sum(c_ref[:, cols] * cross, axis=0, keepdims=True)
+        left = g_full[gram_rows + j : gram_rows + j + 1, :] - explained
         norm_ref[:, cols] = jnp.sqrt(jnp.maximum(left, 0.0) / points_total)
 
 
-def solve_step(packed, image, residual_in, points_total):
+def finish_step(image, residual_in):
+    n_row, n_col = lax.axis_size("row"), lax.axis_size("col")
     width = residual_in.shape[1]
+    tiles = width // LANES
+    gram_total = padded(tiles * (tiles + 1) // 2 * LANES + SUB, n_row * n_col, GRAM_STREAMS)
+    cross_total = padded(tiles * width, n_row * n_col, CROSS_STREAMS)
+    steps = len(stream_orders(n_row, n_col, 1)[0])
     vmem = pl.BlockSpec(memory_space=pltpu.VMEM)
     new_residual, norms = pl.pallas_call(
-        functools.partial(solve_kernel, points_total),
+        functools.partial(finish_kernel, n_row, n_col),
         out_shape=(
             jax.ShapeDtypeStruct(residual_in.shape, jnp.float32),
             jax.ShapeDtypeStruct((1, width), jnp.float32),
         ),
-        in_specs=[vmem] * 3,
+        in_specs=[vmem] * 2,
         out_specs=(vmem, vmem),
-        scratch_shapes=[
-            pltpu.VMEM((width, width), jnp.float32),
-            pltpu.VMEM((width, width), jnp.float32),
-        ],
-        name="solve_all",
-    )(packed, image, residual_in)
+        scratch_shapes=[pltpu.VMEM((gram_total, LANES), jnp.float32)] * 3
+        + [pltpu.VMEM((cross_total, LANES), jnp.float32)] * 3
+        + [pltpu.VMEM((width, width), jnp.float32)] * 2
+        + [pltpu.VMEM((width, LANES), jnp.float32)]
+        + [pltpu.SemaphoreType.DMA((GRAM_STREAMS, steps))] * 4
+        + [pltpu.SemaphoreType.DMA((CROSS_STREAMS, steps))] * 4,
+        compiler_params=pltpu.CompilerParams(collective_id=1, has_side_effects=True),
+        name="finish_all",
+    )(image, residual_in)
     return new_residual, norms[0]
 
 
@@ -478,9 +472,7 @@
     image = local_image(
         coords, residual_in, link_mask, compress, expand, level_gain, level_couple, partner_perm
     )
-    points_total = coords.shape[1] * lax.axis_size("row") * lax.axis_size("col")
-    packed = global_sum(image, residual_in)
-    return solve_step(packed, image, residual_in, points_total)
+    return finish_step(image, residual_in)
 
 
 def solution(mesh):

time: 133 us -> 144 us (1.083)
  Pallas kernels: 130 us -> 138 us
  local copies, waits for them, and re-layouts: 2.69 us -> 5.62 us
    pallas_call x2 -> x1, Pallas kernels: 74.3 us -> 82.2 us  [finish_step(): pl.pallas_call(functools.partial(finish_kernel, n_row, n_col), out_shape=...]
    unnamed x2 -> x4, local copies, waits for them, and re-layouts: 2.69 us -> 5.62 us
where the time goes in v2:
time: 144 us
  Pallas kernels  138 us (96%)
  local copies, waits for them, and re-layouts  5.62 us (4%)
    pallas_call x1, Pallas kernels, finish_step(): pl.pallas_call(functools.partial(finish_kernel, n_row, n_col), out_shape=...  82.2 us
    pallas_call x1, Pallas kernels, local_image(): pl.pallas_call(functools.partial(image_kernel, n_row, n_col), out_shape=j...  55.3 us
    unnamed x4, local copies, waits for them, and re-layouts  5.62 us

profile of v2, /device:TPU:0, one launch (start us, length us, event | category | flops | bytes accessed | tf_op | source)
XLA Modules:
  0.0 143.8 jit_solution(10224118642367948651)
XLA Ops:
  0.6 1.3 copy.11.perm_ref
  1.9 1.4 copy.10
  3.3 55.3 %image_all.1.image_ref = f32[128,512]{1,0:T(8,128)} custom-call(f32[3,128]{1,0:T(4,128)} %coords_ref.1, f32[128,3]{1,0:T(8,128)} %bitcast.2, f32[128,512]{1,0:T(8,128)} %res_ref.3, s32[1,2]{1,0:T(1,128)} %mask_ref.1, f32[128,256]{1,0:T(8,128)} %comp_ref.1, f32[128,256]{1,0:T(8,128)} %exp_ref.1, f32[1,1280]{1,0:T(1,128)} %gain_ref.1, f32[256,1280]{1,0:T(8,128)} %couple_ref.1, ...), custom_call_target="tpu_custom_call" | custom-call | tf_op jit(solution)/shard_map/image_all/pallas_call | solution.py:441
  58.7 82.2 %finish_all.1 = (f32[128,512]{1,0:T(8,128)}, f32[1,512]{1,0:T(1,128)}) custom-call(f32[128,512]{1,0:T(8,128)} %image_all.1.image_ref, f32[128,512]{1,0:T(8,128)} %res_ref.3), custom_call_target="tpu_custom_call" | custom-call | tf_op jit(solution)/shard_map/finish_all/pallas_call | solution.py:261
  140.9 1.7 %copy.14 = f32[128,512]{1,0:T(8,128)} copy(f32[128,512]{1,0:T(8,128)} %get-tuple-element.8) | data formatting | bytes 524288
  142.6 1.3 copy.15

commit v3 on v2

--- a/solution.py
+++ b/solution.py
@@ -55,9 +55,9 @@
 def stream_orders(n_row, n_col, streams):
     col_bits = [("col", b) for b in range(n_col.bit_length() - 1)]
     row_bits = [("row", b) for b in range(n_row.bit_length() - 1)]
-    lead = col_bits[1:] + row_bits[:1]
-    tail = col_bits[:1] + row_bits[1:]
-    return [lead[s:] + lead[:s] + tail for s in range(streams)]
+    core, side = col_bits[:1], col_bits[1:]
+    lead = side + row_bits[:1]
+    return [core + lead[s:] + lead[:s] + row_bits[1:] for s in range(streams)]
 
 
 def bit_of(step):
@@ -208,14 +208,27 @@
         g_ref[i * LANES : (i + 1) * LANES, j * LANES : (j + 1) * LANES] = g_full[
             slot * LANES : (slot + 1) * LANES, :
         ]
-    panels = LANES // SUB
+    steps = len(c_orders[0])
+    quota = [3, 3] + [1] * (steps - 3) + [2]
+    quota = quota + quota[::-1]
+    done = [0]
+
+    def tick():
+        done[0] += 1
+        if quota and done[0] >= quota[0]:
+            quota.pop(0)
+            done[0] = 0
+            next(cross_sum, None)
+
+    pieces = 4
+    panels = LANES // SUB // pieces
     for k in range(tiles):
         lo, hi = k * LANES, (k + 1) * LANES
-        inverse = invert_panels(g_ref[lo:hi, lo:hi], panels // 2)
-        next(cross_sum, None)
-        inverse = invert_panels(inverse, panels - panels // 2)
+        inverse = g_ref[lo:hi, lo:hi]
+        for _ in range(pieces):
+            inverse = invert_panels(inverse, panels)
+            tick()
         inv_ref[lo:hi, :] = inverse
-        next(cross_sum, None)
         if hi < width:
             link = g_ref[lo:hi, hi:]
             right = matmul_hi(inverse, link)
@@ -225,7 +238,7 @@
                     link[:, a - hi : b - hi], right[:, a - hi :]
                 )
             g_ref[lo:hi, hi:] = right
-            next(cross_sum, None)
+            tick()
     for _ in cross_sum:
         pass
 

time: 144 us -> 134 us (0.931)
  Pallas kernels: 138 us -> 127 us
    pallas_call x1, Pallas kernels: 82.2 us -> 72.1 us  [finish_step(): pl.pallas_call(functools.partial(finish_kernel, n_row, n_col), out_shape=...]
where the time goes in v3:
time: 134 us
  Pallas kernels  127 us (95%)
  local copies, waits for them, and re-layouts  5.62 us (4%)
    pallas_call x1, Pallas kernels, finish_step(): pl.pallas_call(functools.partial(finish_kernel, n_row, n_col), out_shape=...  72.1 us
    pallas_call x1, Pallas kernels, local_image(): pl.pallas_call(functools.partial(image_kernel, n_row, n_col), out_shape=j...  55.3 us
    unnamed x4, local copies, waits for them, and re-layouts  5.62 us

profile of v3, /device:TPU:0, one launch (start us, length us, event | category | flops | bytes accessed | tf_op | source)
XLA Modules:
  0.0 133.7 jit_solution(7711909279243392817)
XLA Ops:
  0.6 1.3 copy.11.perm_ref
  1.9 1.4 %copy.10 = f32[3,128]{0,1:T(8,128)} copy(f32[3,128]{1,0:T(4,128)} %coords_ref.1) | data formatting | bytes 3072 | tf_op args[0]
  3.3 55.3 %image_all.1.image_ref = f32[128,512]{1,0:T(8,128)} custom-call(f32[3,128]{1,0:T(4,128)} %coords_ref.1, f32[128,3]{1,0:T(8,128)} %bitcast.2, f32[128,512]{1,0:T(8,128)} %res_ref.3, s32[1,2]{1,0:T(1,128)} %mask_ref.1, f32[128,256]{1,0:T(8,128)} %comp_ref.1, f32[128,256]{1,0:T(8,128)} %exp_ref.1, f32[1,1280]{1,0:T(1,128)} %gain_ref.1, f32[256,1280]{1,0:T(8,128)} %couple_ref.1, ...), custom_call_target="tpu_custom_call" | custom-call | tf_op jit(solution)/shard_map/image_all/pallas_call | solution.py:454
  58.7 72.1 %finish_all.1 = (f32[128,512]{1,0:T(8,128)}, f32[1,512]{1,0:T(1,128)}) custom-call(f32[128,512]{1,0:T(8,128)} %image_all.1.image_ref, f32[128,512]{1,0:T(8,128)} %res_ref.3), custom_call_target="tpu_custom_call" | custom-call | tf_op jit(solution)/shard_map/finish_all/pallas_call | solution.py:274
  130.8 1.7 %copy.14 = f32[128,512]{1,0:T(8,128)} copy(f32[128,512]{1,0:T(8,128)} %get-tuple-element.8) | data formatting | bytes 524288
  132.5 1.3 copy.15
